TPU v7x, 512 devices: a whole 4x4x16 slice. The times are simulated.
512 devices in a mesh: obs: 16 (over y, x), flux: 32 (over z, core).
Axes of the slice: x: 4, y: 4, z: 16, core: 2. Of those that a mesh axis runs over, the one named last changes fastest.
Arguments:
- ensemble: bfloat16 [131072, 256], P(('obs', 'flux')), may hold values from -6 to 6
- footprint: bfloat16 [256, 32, 8, 128, 128], P('obs', 'flux'), may hold values from -0.046875 to 0.046875
- tile_index: int32 [256, 32, 8], P('obs', 'flux'), may hold values from 0 to 31, as said below
- tile_count: int32 [256, 32], P('obs', 'flux'), may hold values from 1 to 8, as said below
- observed: float32 [32768], P(('obs', 'flux')), may hold values from -8 to 8
- obs_sigma: float32 [32768], P(('obs', 'flux')), may hold values from 3 to 30
Outputs:
- posterior: bfloat16 [131072, 256], P(('obs', 'flux'))
Inputs may be any that keep to these rules, and one draw needn't show every extreme that they name: `tile_index`: the 8 tiles of one block and region are different. `tile_count`: some block and region uses all 8 slots.
All inputs are finite; a program needn't handle non-finite values.
Results may differ from a plain program's by a relative error of at most 0.0095.
Values may be sent and summed in bfloat16 or wider, within the bound.
A program may use at most 64 MiB of HBM per device.

v0:
```python
import jax
import jax.numpy as jnp
from jax import lax
from jax.sharding import Mesh
from jax.sharding import PartitionSpec as P

OBS = ("obs_0", "obs_1")
FLUX = ("flux_0", "flux_1")
OBS_FLUX = ("obs_0", "obs_1", "flux_0", "flux_1")


def from_everyone(x, axis):
    copies = jnp.broadcast_to(x, (lax.axis_size(axis), *x.shape))
    return lax.all_to_all(copies, axis, split_axis=0, concat_axis=0, tiled=True)


def in_order(tiles, dim):
    tiles = jnp.moveaxis(tiles, 0, dim)
    dims = tiles.shape
    return tiles.reshape(*dims[:dim], dims[dim] * dims[dim + 1], *dims[dim + 2 :])


def collect(x, axis, dim):
    tiles = from_everyone(x, axis)
    return in_order(tiles, dim)


def sum_in_order(tiles, axes, order):
    inside = tiles.shape[1:]
    tiles = tiles.reshape(*(lax.axis_size(a) for a in axes), *inside)
    tiles = jnp.moveaxis(tiles, order, range(len(axes))).reshape(-1, *inside)
    for k in order:
        tiles = lax.psum_scatter(tiles, axes[k], scatter_dimension=0, tiled=True)
    return tiles[0]


def cut_along(x, dim, devices):
    dims = x.shape
    tiles = x.reshape(*dims[:dim], devices, dims[dim] // devices, *dims[dim + 1 :])
    return jnp.moveaxis(tiles, dim, 0)


def scatter_axes(x, axes, order, dim):
    devices = lax.axis_size(axes)
    return sum_in_order(cut_along(x, dim, devices), axes, order)


def padded_to(lines, devices):
    spare = -lines.shape[0] % devices
    if not spare:
        return lines
    return jnp.concatenate([lines, jnp.zeros((spare, *lines.shape[1:]), lines.dtype)])


def gathered_by_axis(x, axes, dim):
    far, near = axes
    tiles = from_everyone(from_everyone(x, far), near)
    return in_order(tiles.swapaxes(0, 1).reshape(-1, *x.shape), dim)


def summed_on_arrival(x, axis, dim):
    tiles = cut_along(x, dim, lax.axis_size(axis))
    arrived = lax.all_to_all(tiles, axis, split_axis=0, concat_axis=0, tiled=True)
    return arrived.sum(axis=0)


def sum_in_two_steps(x, axes, dim):
    far, near = axes
    tiles = cut_along(x, dim, lax.axis_size(far))
    nearer = summed_on_arrival(tiles, near, dim + 1)
    arrived = lax.all_to_all(nearer, far, split_axis=0, concat_axis=0, tiled=True)
    return arrived.sum(axis=0)


def nested_sum(x, axes):
    padded = padded_to(x, lax.axis_size(axes[0]) * lax.axis_size(axes[1]))
    whole = gathered_by_axis(sum_in_two_steps(padded, axes, 0), axes, 0)
    return lax.slice_in_dim(whole, 0, len(x)).reshape(x.shape)


def together(arrays, axis):
    ends = [0]
    for a in arrays:
        ends.append(ends[-1] + a.size)
    so_far = nested_sum(jnp.concatenate([a.ravel() for a in arrays]), axis)
    return tuple((so_far[b:e].reshape(a.shape) for a, b, e in zip(arrays, ends, ends[1:])))


def per_device(ensemble, footprint, tile_index, tile_count, observed, obs_sigma):
    members = ensemble.shape[1]
    tile_size = footprint.shape[-1]
    slots = footprint.shape[2]
    region_block = collect(ensemble, OBS, 0)
    region_tiles = region_block.reshape(-1, tile_size, members)
    picked = region_tiles[tile_index[:, 0, :]]
    occupied = jnp.arange(slots, dtype=jnp.int32)[None, :] < tile_count[:, 0][:, None]
    masked = jnp.where(occupied[:, :, None, None], footprint[:, 0], jnp.zeros((), jnp.bfloat16))
    partial_value = jnp.einsum("bsij,bsjm->bim", masked, picked, preferred_element_type=jnp.float32)
    partial_value = partial_value.reshape(-1, members)
    own_rows = scatter_axes(partial_value.astype(jnp.bfloat16), FLUX, (1, 0), 0).astype(jnp.float32)
    mean_sim = jnp.mean(own_rows, axis=1)
    scaled = (own_rows - mean_sim[:, None]) / obs_sigma[:, None]
    innovation = (observed - mean_sim) / obs_sigma
    gram_local = jnp.dot(scaled.T, scaled, precision=lax.Precision.HIGHEST)
    proj_local = jnp.dot(innovation, scaled, precision=lax.Precision.HIGHEST)
    gram, proj = together((gram_local, proj_local), (("obs_0", "obs_1"), ("flux_0", "flux_1")))
    eye = jnp.eye(members, dtype=jnp.float32)
    system = (members - 1.0) * eye + gram
    factor = jnp.linalg.cholesky(system)
    solved = jax.scipy.linalg.cho_solve(
        (factor, True), jnp.concatenate([proj[:, None], gram], axis=1)
    )
    weights = eye - 0.5 * solved[:, 1:] + solved[:, 0][:, None]
    prior = ensemble.astype(jnp.float32)
    prior_mean = jnp.mean(prior, axis=1)
    anomaly = prior - prior_mean[:, None]
    posterior = prior_mean[:, None] + jnp.dot(anomaly, weights, precision=lax.Precision.HIGHEST)
    return posterior.astype(jnp.bfloat16)


def solution(mesh):
    finer = Mesh(mesh.devices.reshape(4, 4, 16, 2), ("obs_0", "obs_1", "flux_0", "flux_1"))
    placed = (
        P(OBS_FLUX, None),
        P(OBS, FLUX, None, None, None),
        P(OBS, FLUX, None),
        P(OBS, FLUX),
        P(OBS_FLUX),
        P(OBS_FLUX),
    )
    return jax.shard_map(
        per_device, mesh=finer, in_specs=placed, out_specs=P(OBS_FLUX, None), check_vma=False
    )
```

profile of v0, /device:TPU:1, one launch (start us, length us, event | category | flops | bytes accessed | tf_op | source)
XLA Modules:
  0.0 339.1 jit_solution(9560417995398442142)
XLA Ops:
  6.5 0.0 copy-start.1
  6.5 2.5 broadcast_in_dim.38
  9.0 7.6 %all-to-all-start = ((bf16[16,256,256]{2,1,0:T(8,128)(2,1)}), bf16[16,256,256]{2,1,0:T(8,128)(2,1)S(1)}, u32[]{:S(2)}, u32[]{:S(2)}) async-start(bf16[16,256,256]{2,1,0:T(8,128)(2,1)} %broadcast_in_dim.38), calls=%async_computation | async-start | bytes 4194304 | tf_op jit(solution)/shard_map/all_to_all | solution.py:14
  16.6 0.0 reduce-scatter.3.cloned.1.call-start
  16.7 0.0 copy-done.1
  16.7 0.1 copy.25
  16.7 0.1 reshape.149
  16.9 0.0 copy-done.3
  16.9 0.1 iota_compare_fusion.5
  16.9 25.0 %all-to-all-done = bf16[16,256,256]{2,1,0:T(8,128)(2,1)S(1)} async-done(((bf16[16,256,256]{2,1,0:T(8,128)(2,1)}), bf16[16,256,256]{2,1,0:T(8,128)(2,1)S(1)}, u32[]{:S(2)}, u32[]{:S(2)}) %all-to-all-start) | async-done | bytes 2097184 | tf_op jit(solution)/shard_map/all_to_all | solution.py:14
  41.9 6.6 %gather_fusion = bf16[128,128,256]{2,1,0:T(8,128)(2,1)} fusion(bf16[32,128,256]{2,1,0:T(8,128)(2,1)S(1)} %bitcast.79, s32[1024]{0:T(1024)S(1)} %pad_clamp_fusion), kind=kCustom, calls=%fused_computation | custom fusion | bytes 16777728 | tf_op jit(solution)/shard_map/gather | solution.py:95
  48.5 6.0 %bitcast_convert_fusion = bf16[16,128,256]{2,1,0:T(8,128)(2,1)S(1)} fusion(bf16[16,8,128,256]{3,2,1,0:T(8,128)(2,1)} %bitcast.80, bf16[16,1,8,128,128]{4,3,2,1,0:T(8,128)(2,1)} %param.7, pred[16,8]{1,0:T(8,128)(4,1)S(1)} %iota_compare_fusion.5), kind=kOutput, calls=%fused_computation.6 | convolution fusion | flops 1076363264 | bytes 13631616 | tf_op jit(solution)/shard_map/bsij,bsjm->bim/dot_general | solution.py:98
  54.4 0.0 copy-start.4
  54.5 1.1 copy.26
  55.6 0.0 reduce-scatter.3.cloned.1.call-update
  55.6 0.0 reduce-scatter.5.cloned.1.call-start
  55.6 28.1 %reduce-scatter.3.cloned.1.call-done = bf16[16,64,256]{2,1,0:T(8,128)(2,1)} async-done(((bf16[32,64,256]{2,1,0:T(8,128)(2,1)}), bf16[16,64,256]{2,1,0:T(8,128)(2,1)}) %reduce-scatter.3.cloned.1.call-update) | async-done | bytes 524304 | tf_op jit(solution)/shard_map/reduce_scatter | solution.py:33
  83.7 0.0 reduce-scatter.5.cloned.1.call-update
  83.7 62.2 %reduce-scatter.5.cloned.1.call-done = bf16[1,64,256]{2,1,0:T(8,128)(2,1)} async-done(((bf16[16,64,256]{2,1,0:T(8,128)(2,1)}), bf16[1,64,256]{2,1,0:T(8,128)(2,1)}) %reduce-scatter.5.cloned.1.call-update) | async-done | bytes 32784 | tf_op jit(solution)/shard_map/reduce_scatter | solution.py:33
  145.9 0.9 convert_reduce_fusion.1
  146.8 0.0 copy-done.2
  146.8 1.3 convolution_bitcast_fusion
  148.2 0.1 copy.39
  148.3 0.0 copy-done.4
  148.3 1.0 fusion.26
  149.3 0.6 reshape_reshape.11
  149.9 0.3 copy.27
  150.2 53.4 %all_to_all.33 = f32[32,16,129]{2,1,0:T(8,128)S(1)} all-to-all(f32[32,16,129]{2,1,0:T(8,128)S(1)} %copy.27), channel_id=1, replica_groups=mesh['obs_0'=4,'obs_1'=4,'flux_0'=16,'flux_1'=2] {'flux_0','flux_1'}, dimensions={0} | all-to-all | bytes 528384 | tf_op jit(solution)/shard_map/all_to_all | solution.py:63
  203.6 0.1 reduce_sum.38
  203.6 12.8 %all_to_all.34 = f32[16,1,129]{2,1,0:T(1,128)S(1)} all-to-all(f32[16,1,129]{2,1,0:T(1,128)S(1)} %all_to_all.23), channel_id=1, replica_groups=mesh['obs_0'=4,'obs_1'=4,'flux_0'=16,'flux_1'=2] {'obs_0','obs_1'}, dimensions={0} | all-to-all | bytes 16512 | tf_op jit(solution)/shard_map/all_to_all | solution.py:71
  216.4 9.5 %all_to_all.35 = f32[16,1,129]{2,1,0:T(1,128)S(1)} all-to-all(f32[16,1,129]{2,1,0:T(1,128)S(1)} %broadcast_in_dim.40), channel_id=1, replica_groups=mesh['obs_0'=4,'obs_1'=4,'flux_0'=16,'flux_1'=2] {'obs_0','obs_1'}, dimensions={0} | all-to-all | bytes 16512 | tf_op jit(solution)/shard_map/all_to_all | solution.py:14
  225.9 0.9 broadcast_in_dim.41
  226.8 6.6 %all-to-all-start.4 = ((f32[32,16,129]{2,1,0:T(8,128)}), f32[32,16,129]{2,1,0:T(8,128)S(1)}, u32[]{:S(2)}, u32[]{:S(2)}) async-start(f32[32,16,129]{2,1,0:T(8,128)} %broadcast_in_dim.41), calls=%async_computation.6 | async-start | bytes 1048576 | tf_op jit(solution)/shard_map/all_to_all | solution.py:14
  233.4 0.0 copy-done
  233.4 0.1 convert_reduce_fusion
  233.5 33.4 %all-to-all-done.4 = f32[32,16,129]{2,1,0:T(8,128)S(1)} async-done(((f32[32,16,129]{2,1,0:T(8,128)}), f32[32,16,129]{2,1,0:T(8,128)S(1)}, u32[]{:S(2)}, u32[]{:S(2)}) %all-to-all-start.4) | async-done | bytes 264224 | tf_op jit(solution)/shard_map/all_to_all | solution.py:14
  266.9 0.3 copy.28
  267.2 0.5 slice.80
  267.8 0.1 copy.29
  267.9 0.1 fusion.9
  268.0 11.7 %cholesky.49 = f32[128,128]{1,0:T(8,128)S(1)} custom-call(f32[128,128]{1,0:T(8,128)S(1)} %cholesky.115), custom_call_target="Cholesky" | custom-call | tf_op jit(solution)/shard_map/jit(cholesky)/cholesky | solution.py:109
  279.8 0.4 reshape_reshape.12
  280.2 9.8 %custom-call.18 = f32[1,128,128]{1,2,0:T(8,128)S(1)} custom-call(f32[1,128,128]{2,1,0:T(8,128)S(1)} %get-tuple-element.28), custom_call_target="InvertDiagBlocksLowerTriangular" | custom-call | tf_op jit(solution)/shard_map/jit(cholesky)/cholesky | solution.py:109
  290.0 0.2 constant_dynamic-update-slice_fusion.1
  290.2 0.3 convolution_subtract_fusion.2
  290.4 11.7 %cholesky.103 = f32[128,128]{1,0:T(8,128)S(1)} custom-call(f32[128,128]{1,0:T(8,128)S(1)} %convolution_subtract_fusion.2), custom_call_target="Cholesky" | custom-call | tf_op jit(solution)/shard_map/jit(cholesky)/cholesky | solution.py:109
  302.2 0.7 compare_reduce_fusion
  304.2 0.1 triangular_solve.61
  304.3 4.1 %while.1 = (s32[]{:T(128)}, f32[256,256]{1,0:T(8,128)S(1)}, s32[2,2]{1,0:T(2,128)S(1)}, f32[2,128,128]{2,1,0:T(8,128)S(1)}, s32[]{:T(128)}) while((s32[]{:T(128)}, f32[256,256]{1,0:T(8,128)S(1)}, s32[2,2]{1,0:T(2,128)S(1)}, f32[2,128,128]{2,1,0:T(8,128)S(1)}, s32[]{:T(128)}) %tuple.24), condition=%wide.while_cond, body=%wide.while_body.sunk | while | flops 2 | bytes 131181 | solution.py:110
  304.3 0.7 fusion.52
  305.0 1.3 bitcast_dynamic-update-slice_fusion.2
  306.3 0.7 fusion.52
  307.0 1.3 bitcast_dynamic-update-slice_fusion.2
  308.3 19.9 %custom-call.19 = f32[2,128,128]{1,2,0:T(8,128)S(1)} custom-call(f32[2,128,128]{2,1,0:T(8,128)S(1)} %get-tuple-element.12), custom_call_target="InvertDiagBlocksLowerTriangular" | custom-call | tf_op jit(solution)/shard_map/jit(_cho_solve)/triangular_solve | solution.py:110
  328.3 0.1 copy.31
  328.4 0.6 fusion.12
  329.0 0.3 convolution_subtract_fusion
  329.3 0.5 fusion.30
  329.8 0.4 fusion.29
  330.2 0.4 convolution_subtract_fusion.1
  330.6 0.1 copy.34
  330.7 0.3 fusion.28
  331.0 0.1 fusion.14
  331.1 1.2 fusion.3
  (24 shorter events, 0.3 us)
Async XLA Ops:
  6.5 10.1 %copy-start.1 = (s32[16,1,8]{0,2,1:T(8,128)S(1)}, s32[16,1,8]{0,2,1:T(8,128)}, u32[]{:S(2)}) copy-start(s32[16,1,8]{0,2,1:T(8,128)} %param.8) | copy-start | bytes 1540
  6.5 10.3 %copy-start.3 = (s32[16,1]{0,1:T(1,128)S(1)}, s32[16,1]{0,1:T(1,128)}, u32[]{:S(2)}) copy-start(s32[16,1]{0,1:T(1,128)} %param.9) | copy-start | bytes 196
  9.0 32.9 %all-to-all-start = ((bf16[16,256,256]{2,1,0:T(8,128)(2,1)}), bf16[16,256,256]{2,1,0:T(8,128)(2,1)S(1)}, u32[]{:S(2)}, u32[]{:S(2)}) async-start(bf16[16,256,256]{2,1,0:T(8,128)(2,1)} %broadcast_in_dim.38), calls=%async_computation | async-start | bytes 4194304 | tf_op jit(solution)/shard_map/all_to_all | solution.py:14
  16.6 67.1 %reduce-scatter.3.cloned.1.call-start = ((), (), s32[]{:S(2)}) async-start(), calls=%async_computation.7 | async-start | bytes 1572864 | tf_op jit(solution)/shard_map/reduce_scatter | solution.py:33
  48.5 98.4 %copy-start.2 = (f32[64]{0:T(128)S(1)}, f32[64]{0:T(128)}, u32[]{:S(2)}) copy-start(f32[64]{0:T(128)} %param.11) | copy-start | bytes 772
  54.4 93.9 %copy-start.4 = (f32[64]{0:T(128)S(1)}, f32[64]{0:T(128)}, u32[]{:S(2)}) copy-start(f32[64]{0:T(128)} %param.10) | copy-start | bytes 772
  55.6 177.9 %copy-start = (bf16[256,256]{1,0:T(8,128)(2,1)S(1)}, bf16[256,256]{1,0:T(8,128)(2,1)}, u32[]{:S(2)}) copy-start(bf16[256,256]{1,0:T(8,128)(2,1)} %param.6) | copy-start | bytes 393220
  55.6 90.4 %reduce-scatter.5.cloned.1.call-start = ((), (), s32[]{:S(2)}) async-start(), calls=%async_computation.8 | async-start | bytes 557056 | tf_op jit(solution)/shard_map/reduce_scatter | solution.py:33
  226.8 40.1 %all-to-all-start.4 = ((f32[32,16,129]{2,1,0:T(8,128)}), f32[32,16,129]{2,1,0:T(8,128)S(1)}, u32[]{:S(2)}, u32[]{:S(2)}) async-start(f32[32,16,129]{2,1,0:T(8,128)} %broadcast_in_dim.41), calls=%async_computation.6 | async-start | bytes 1048576 | tf_op jit(solution)/shard_map/all_to_all | solution.py:14
Sparse Core Ops, SparseCore 0:
  55.7 27.9 reduce-scatter.2
  86.5 59.4 reduce-scatter.4
where the time goes:
time: 340 us; the launch traced here: 339 us
  waiting for transfers between devices  149 us (44%)
  blocking collectives  75.6 us (22%)
  other arithmetic  55.3 us (16%)
  local copies, waits for them, and re-layouts  17.9 us (5%)
  between operations  15 us (4%)
  starting transfers between devices  14.3 us (4%)
  matrix products  12.4 us (4%)
    reduce_scatter x2, waiting for transfers between devices, sum_in_order(): tiles = lax.psum_scatter(tiles, axes[k], scatter_dimension=0, tiled=True)  90.3 us
    all_to_all x2, waiting for transfers between devices, from_everyone(): return lax.all_to_all(copies, axis, split_axis=0, concat_axis=0, tiled=True)  58.3 us
    all_to_all x1, blocking collectives, summed_on_arrival(): lax.all_to_all(tiles, axis, split_axis=0, concat_axis=0, tiled=True)  53.4 us
    another operation x6, other arithmetic, per_device(): factor = jnp.linalg.cholesky(system)  34 us
    another operation x3, other arithmetic, per_device(): jax.scipy.linalg.cho_solve((factor, True), jnp.concatenate([proj[:, None]...  19.9 us
    all_to_all x2, starting transfers between devices, from_everyone(): return lax.all_to_all(copies, axis, split_axis=0, concat_axis=0, tiled=True)  14.2 us
    all_to_all x1, blocking collectives, sum_in_two_steps(): lax.all_to_all(nearer, far, split_axis=0, concat_axis=0, tiled=True)  12.8 us
    all_to_all x1, blocking collectives, from_everyone(): return lax.all_to_all(copies, axis, split_axis=0, concat_axis=0, tiled=True)  9.46 us
  transfers between devices with their start and end apart: 4, of which 4 were waited for; matrix products, arithmetic and copies ran while one was open for 0% of the time, Pallas kernels for 0%

commit v1 on v0

v1 whole, which is shorter than its diff:
```python
import functools

import jax
import jax.numpy as jnp
from jax import lax
from jax.experimental import pallas as pl
from jax.experimental.pallas import tpu as pltpu
from jax.sharding import Mesh
from jax.sharding import PartitionSpec as P

OBS = ("obs_0", "obs_1")
FLUX = ("flux_0", "flux_1")
OBS_FLUX = OBS + FLUX
MESH = pl.DeviceIdType.MESH
F32 = jnp.float32
BF16 = jnp.bfloat16
Z = 16
Q = 4


def update_kernel(
    index_ref, count_ref, ensemble_ref, footprint_ref, observed_ref, sigma_ref,
    gram_ref,
    region, prints, part, pair_out, pair_in, right_out, right_in, left_out, left_in,
    halves, half_in, z_out, z_in, plane_out, plane_in,
    local_sems, hop_send, hop_recv, pair_send, pair_recv,
    right_send, right_recv, left_send, left_recv, half_sems,
    z_send, z_recv, plane_send, plane_recv, share_send, share_recv, give_send, give_recv,
):
    y, x = lax.axis_index("obs_0"), lax.axis_index("obs_1")
    z, c = lax.axis_index("flux_0"), lax.axis_index("flux_1")
    other = 1 - c

    def along_z(step):
        return (y, x, lax.rem(z + step + Z, Z), c)

    def in_plane(dy, dx):
        return (lax.rem(y + dy + Q, Q), lax.rem(x + dx + Q, Q), z, c)

    def hop(first, second):
        return in_plane(c * first + other * second, other * first + c * second)

    def owner(first, second):
        at = hop(first, second)
        return at[0] * Q + at[1]

    partner = (y, x, z, other)
    mine = y * Q + x

    load_prints = pltpu.make_async_copy(footprint_ref, prints, local_sems.at[0])
    load_prints.start()
    own = pltpu.make_async_copy(ensemble_ref, region.at[pl.ds(2 * mine, 2)], local_sems.at[1])
    own.start()

    barrier = pltpu.get_barrier_semaphore()
    pl.semaphore_signal(barrier, inc=1, device_id=partner, device_id_type=MESH)

    @pl.loop(1, Z)
    def _(step):
        pl.semaphore_signal(barrier, inc=1, device_id=along_z(step), device_id_type=MESH)
        pl.semaphore_signal(
            barrier, inc=1, device_id=in_plane(step // Q, lax.rem(step, Q)), device_id_type=MESH
        )

    pl.semaphore_wait(barrier, 2 * Z - 1)

    def piece(src, dst, sem, to):
        return pltpu.make_async_remote_copy(
            src_ref=src, dst_ref=dst, send_sem=hop_send.at[sem], recv_sem=hop_recv.at[sem],
            device_id=to, device_id_type=MESH,
        )

    def arrived(ref, sem):
        piece(ref, ref, sem, partner).wait_recv()

    sent = []

    def send(src, dst, sem, to):
        copy = piece(src, dst, sem, to)
        copy.start()
        sent.append(copy)

    def rows(o):
        return region.at[pl.ds(2 * o, 2)]

    def tile(o, k):
        return region.at[2 * o + k]

    forward, back = hop(1, 0), hop(-1, 0)
    up, down = hop(0, 1), hop(0, -1)

    def rows_at(src, o, k):
        send(src, rows(o), 4 + 4 * k, up)
        send(src, rows(o), 5 + 4 * k, down)

    def pass_on(first, k):
        lower, upper = owner(first, -1), owner(first, 1)
        arrived(rows(lower), 4 + 4 * k)
        send(tile(lower, 0), tile(lower, 0), 6 + 4 * k, up)
        arrived(rows(upper), 5 + 4 * k)
        send(tile(upper, 1), tile(upper, 1), 7 + 4 * k, down)

    send(ensemble_ref, rows(mine), 0, forward)
    send(ensemble_ref, rows(mine), 1, back)
    rows_at(ensemble_ref, mine, 0)
    behind, ahead, across = owner(-1, 0), owner(1, 0), owner(2, 0)
    arrived(rows(behind), 0)
    send(tile(behind, 0), tile(behind, 0), 2, forward)
    rows_at(rows(behind), behind, 1)
    arrived(rows(ahead), 1)
    send(tile(ahead, 1), tile(ahead, 1), 3, back)
    rows_at(rows(ahead), ahead, 2)
    pass_on(0, 0)
    arrived(tile(across, 0), 2)
    arrived(tile(across, 1), 3)
    rows_at(rows(across), across, 3)
    pass_on(-1, 1)
    pass_on(1, 2)
    pass_on(2, 3)
    for k, first in enumerate((0, -1, 1, 2)):
        far = owner(first, 2)
        arrived(tile(far, 0), 6 + 4 * k)
        arrived(tile(far, 1), 7 + 4 * k)
    own.wait()
    load_prints.wait()

    def offset(t):
        s = t // 2
        return jnp.where(lax.rem(t, 2) == 0, 8 - s, 9 + s)

    def pair_copy(t):
        return pltpu.make_async_remote_copy(
            src_ref=pair_out.at[t], dst_ref=pair_in.at[t], send_sem=pair_send.at[t],
            recv_sem=pair_recv.at[t], device_id=partner, device_id_type=MESH,
        )

    def block(t):
        b = lax.rem(z + offset(t), Z)
        count = count_ref[b]
        lhs, rhs = [], []
        for s in range(8):
            values = prints[b, s]
            lhs.append(jnp.where(s < count, values, jnp.zeros_like(values)))
            at = index_ref[b, s]
            rhs.append(region[at])
        total = jnp.dot(
            jnp.concatenate(lhs, axis=1), jnp.concatenate(rhs, axis=0), preferred_element_type=F32
        )
        part[t] = jnp.where(c == 0, total[:64], total[64:])
        pair_out[t] = jnp.where(c == 0, total[64:], total[:64]).astype(BF16)
        pair_copy(t).start()

    def right_copy(s):
        return pltpu.make_async_remote_copy(
            src_ref=right_out.at[s], dst_ref=right_in.at[s + 1], send_sem=right_send.at[s],
            recv_sem=right_recv.at[s + 1], device_id=along_z(1), device_id_type=MESH,
        )

    def left_copy(s):
        return pltpu.make_async_remote_copy(
            src_ref=left_out.at[s], dst_ref=left_in.at[s + 1], send_sem=left_send.at[s],
            recv_sem=left_recv.at[s + 1], device_id=along_z(-1), device_id_type=MESH,
        )

    right_in[0] = jnp.zeros_like(right_in[0])
    left_in[0] = jnp.zeros_like(left_in[0])

    def own_sum(t):
        pair_copy(t).wait_recv()
        return part[t] + pair_in[t].astype(F32)

    @pl.loop(0, 9)
    def _(s):
        @pl.when(s < 8)
        def _():
            block(2 * s)
            block(2 * s + 1)

        @pl.when(s >= 1)
        def _():
            now = s - 1
            rightward = own_sum(2 * now)

            @pl.when(now >= 1)
            def _():
                right_copy(now - 1).wait_recv()

            right_out[now] = (rightward + right_in[now].astype(F32)).astype(BF16)
            right_copy(now).start()

            @pl.when(now < 7)
            def _():
                leftward = own_sum(2 * now + 1)

                @pl.when(now >= 1)
                def _():
                    left_copy(now - 1).wait_recv()

                left_out[now] = (leftward + left_in[now].astype(F32)).astype(BF16)
                left_copy(now).start()

    evolved = own_sum(15)
    left_copy(6).wait_recv()
    evolved = evolved + left_in[7].astype(F32)
    right_copy(7).wait_recv()
    evolved = evolved + right_in[8].astype(F32)

    lines = lax.broadcasted_iota(jnp.int32, (64, 64), 0)
    columns = lax.broadcasted_iota(jnp.int32, (64, 64), 1)

    def upright(row):
        return jnp.sum(jnp.where(lines == columns, row, 0.0), axis=1, keepdims=True)

    sigma = upright(sigma_ref[...])
    mean_sim = jnp.mean(evolved, axis=1, keepdims=True)
    scaled = (evolved - mean_sim) / sigma
    innovation = (upright(observed_ref[...]) - mean_sim) / sigma
    gram = lax.dot_general(
        scaled, scaled, (((0,), (0,)), ((), ())), precision=lax.Precision.HIGHEST,
        preferred_element_type=F32,
    )
    proj = jnp.sum(innovation * scaled, axis=0, keepdims=True)
    halves[0] = gram[:128]
    halves[1, :, :128] = gram[128:, 128:]
    line = lax.broadcasted_iota(jnp.int32, (128, 128), 0)
    halves[1, :, 128:] = jnp.where(
        line == 0, proj[:, :128], jnp.where(line == 1, proj[:, 128:], 0.0)
    )

    half_copy = pltpu.make_async_remote_copy(
        src_ref=halves.at[other], dst_ref=half_in, send_sem=half_sems.at[0],
        recv_sem=half_sems.at[1], device_id=partner, device_id_type=MESH,
    )
    half_copy.start()
    half_copy.wait_recv()
    z_out[...] = (halves[c] + half_in[...]).reshape(Z, 8, 256)

    def z_copy(t):
        step = offset(t)
        return pltpu.make_async_remote_copy(
            src_ref=z_out.at[lax.rem(z + step, Z)], dst_ref=z_in.at[t], send_sem=z_send.at[t],
            recv_sem=z_recv.at[t], device_id=along_z(step), device_id_type=MESH,
        )

    @pl.loop(0, Z - 1)
    def _(t):
        z_copy(t).start()

    def add_z(i, total):
        t = Z - 2 - i
        z_copy(t).wait_recv()
        return total + z_in[t]

    plane_out[...] = lax.fori_loop(0, Z - 1, add_z, z_out[z])

    def plane_copy(t):
        return pltpu.make_async_remote_copy(
            src_ref=plane_out, dst_ref=plane_in.at[t], send_sem=plane_send.at[t],
            recv_sem=plane_recv.at[t], device_id=in_plane(t // Q, lax.rem(t, Q)), device_id_type=MESH,
        )

    @pl.loop(1, Z)
    def _(t):
        plane_copy(t).start()

    def add_plane(t, total):
        plane_copy(t).wait_recv()
        return total + plane_in[t]

    whole = lax.fori_loop(1, Z, add_plane, plane_out[...])
    gram_ref[c, z] = whole

    def share_copy(t, at):
        return pltpu.make_async_remote_copy(
            src_ref=gram_ref.at[c, at], dst_ref=gram_ref.at[c, at], send_sem=share_send.at[t],
            recv_sem=share_recv.at[t], device_id=along_z(offset(t)), device_id_type=MESH,
        )

    def give_copy(t, half, at):
        return pltpu.make_async_remote_copy(
            src_ref=gram_ref.at[half, at], dst_ref=gram_ref.at[half, at], send_sem=give_send.at[t],
            recv_sem=give_recv.at[t], device_id=partner, device_id_type=MESH,
        )

    @pl.loop(0, Z - 1)
    def _(t):
        share_copy(t, z).start()

    give_copy(15, c, z).start()

    @pl.loop(0, Z - 1)
    def _(i):
        t = Z - 2 - i
        at = lax.rem(z - offset(t) + Z, Z)
        share_copy(t, at).wait_recv()
        give_copy(t, c, at).start()

    @pl.loop(0, Z)
    def _(i):
        t = Z - 1 - i
        at = lax.rem(z - offset(t) + Z, Z)
        give_copy(t, other, at).wait_recv()

    for copy in sent:
        copy.wait_send()
    half_copy.wait_send()

    @pl.loop(0, Z)
    def _(t):
        pair_copy(t).wait_send()
        give_copy(t, c, z).wait_send()

    @pl.loop(0, 8)
    def _(s):
        right_copy(s).wait_send()

    @pl.loop(0, 7)
    def _(s):
        left_copy(s).wait_send()

    @pl.loop(0, Z - 1)
    def _(t):
        z_copy(t).wait_send()
        plane_copy(t + 1).wait_send()
        share_copy(t, z).wait_send()


def summed_gram(ensemble, footprint, tile_index, tile_count, observed, obs_sigma):
    dma = pltpu.SemaphoreType.DMA
    vmem = pltpu.VMEM
    return pl.pallas_call(
        update_kernel,
        out_shape=jax.ShapeDtypeStruct((2, Z, 8, 256), F32),
        in_specs=[
            pl.BlockSpec(memory_space=pltpu.SMEM),
            pl.BlockSpec(memory_space=pltpu.SMEM),
            pl.BlockSpec(memory_space=pl.ANY),
            pl.BlockSpec(memory_space=pl.ANY),
            pl.BlockSpec(memory_space=vmem),
            pl.BlockSpec(memory_space=vmem),
        ],
        out_specs=pl.BlockSpec(memory_space=vmem),
        scratch_shapes=[
            vmem((32, 128, 256), BF16),
            vmem((16, 8, 128, 128), BF16),
            vmem((16, 64, 256), F32),
            vmem((16, 64, 256), BF16),
            vmem((16, 64, 256), BF16),
            vmem((8, 64, 256), BF16),
            vmem((9, 64, 256), BF16),
            vmem((7, 64, 256), BF16),
            vmem((8, 64, 256), BF16),
            vmem((2, 128, 256), F32),
            vmem((128, 256), F32),
            vmem((Z, 8, 256), F32),
            vmem((Z, 8, 256), F32),
            vmem((8, 256), F32),
            vmem((Z, 8, 256), F32),
            dma((2,)),
            dma((20,)),
            dma((20,)),
            dma((16,)),
            dma((16,)),
            dma((8,)),
            dma((9,)),
            dma((7,)),
            dma((8,)),
            dma((2,)),
            dma((Z,)),
            dma((Z,)),
            dma((Z,)),
            dma((Z,)),
            dma((Z,)),
            dma((Z,)),
            dma((Z,)),
            dma((Z,)),
        ],
        compiler_params=pltpu.CompilerParams(collective_id=0, has_side_effects=True),
    )(
        tile_index.reshape(16, 8), tile_count.reshape(16), ensemble.reshape(2, 128, 256),
        footprint.reshape(16, 8, 128, 128), observed.reshape(1, 64), obs_sigma.reshape(1, 64),
    )


def per_device(ensemble, footprint, tile_index, tile_count, observed, obs_sigma):
    members = ensemble.shape[1]
    packed = summed_gram(ensemble, footprint, tile_index, tile_count, observed, obs_sigma)
    packed = packed.reshape(2, 128, 256)
    top, corner = packed[0], packed[1, :, :128]
    proj = packed[1, :2, 128:].reshape(256)
    gram = jnp.concatenate([top, jnp.concatenate([top[:, 128:].T, corner], axis=1)], axis=0)
    eye = jnp.eye(members, dtype=jnp.float32)
    system = (members - 1.0) * eye + gram
    factor = jnp.linalg.cholesky(system)
    solved = jax.scipy.linalg.cho_solve(
        (factor, True), jnp.concatenate([proj[:, None], gram], axis=1)
    )
    weights = eye - 0.5 * solved[:, 1:] + solved[:, 0][:, None]
    prior = ensemble.astype(jnp.float32)
    prior_mean = jnp.mean(prior, axis=1)
    anomaly = prior - prior_mean[:, None]
    posterior = prior_mean[:, None] + jnp.dot(anomaly, weights, precision=lax.Precision.HIGHEST)
    return posterior.astype(jnp.bfloat16)


def solution(mesh):
    finer = Mesh(mesh.devices.reshape(4, 4, 16, 2), OBS_FLUX)
    placed = (
        P(OBS_FLUX, None),
        P(OBS, FLUX, None, None, None),
        P(OBS, FLUX, None),
        P(OBS, FLUX),
        P(OBS_FLUX),
        P(OBS_FLUX),
    )
    return jax.shard_map(
        per_device, mesh=finer, in_specs=placed, out_specs=P(OBS_FLUX, None), check_vma=False
    )
```

time: 340 us -> 158 us (0.46)
  waiting for transfers between devices: 149 us -> 0 us
  Pallas kernels: 0 us -> 89 us
  blocking collectives: 75.6 us -> 0 us
  starting transfers between devices: 14.3 us -> 0 us
  between operations: 15 us -> 1.46 us
  local copies, waits for them, and re-layouts: 17.9 us -> 8.41 us
  matrix products: 12.4 us -> 3.99 us
    reduce_scatter x2 -> x0, waiting for transfers between devices: 90.3 us -> none  [sum_in_order(): tiles = lax.psum_scatter(tiles, axes[k], scatter_dimension=0, tiled=True)]
    pallas_call x0 -> x1, Pallas kernels: none -> 89 us  [summed_gram(): pl.pallas_call(update_kernel, out_shape=jax.ShapeDtypeStruct((2, Z, 8, 25...]
    all_to_all x3 -> x0, blocking collectives: 75.6 us -> none  [the longest x1 53.4 us: summed_on_arrival(): lax.all_to_all(tiles, axis, split_axis=0, concat_axis=0, tiled=True)]
    all_to_all x2 -> x0, waiting for transfers between devices: 58.3 us -> none  [from_everyone(): return lax.all_to_all(copies, axis, split_axis=0, concat_axis=0, tiled=True)]
    all_to_all x2 -> x0, starting transfers between devices: 14.2 us -> none  [from_everyone(): return lax.all_to_all(copies, axis, split_axis=0, concat_axis=0, tiled=True)]
    dot_general x3 -> x0, matrix products: 8.27 us -> none  [the longest x1 5.98 us: per_device(): jnp.einsum('bsij,bsjm->bim', masked, picked, preferred_element_type=jnp.f...]
    gather x1 -> x0, local copies, waits for them, and re-layouts: 6.55 us -> none  [per_device(): picked = region_tiles[tile_index[:, 0, :]]]
    broadcast_in_dim x5 -> x0, local copies, waits for them, and re-layouts: 3.48 us -> none  [the longest x3 3.35 us: from_everyone(): copies = jnp.broadcast_to(x, (lax.axis_size(axis), *x.shape))]
  transfers between devices with their start and end apart: 4 -> 0, of which waited for: 4 -> 0; matrix products, arithmetic and copies ran while one was open for 0% -> 0% of each run, Pallas kernels for 0% -> 0%
where the time goes in v1:
time: 158 us; the launch traced here: 157 us
  Pallas kernels  89 us (56%)
  other arithmetic  54.4 us (34%)
  local copies, waits for them, and re-layouts  8.41 us (5%)
  matrix products  3.99 us (3%)
    pallas_call x1, Pallas kernels, summed_gram(): pl.pallas_call(update_kernel, out_shape=jax.ShapeDtypeStruct((2, Z, 8, 25...  89 us
    another operation x6, other arithmetic, per_device(): factor = jnp.linalg.cholesky(system)  34 us
    another operation x3, other arithmetic, per_device(): jax.scipy.linalg.cho_solve((factor, True), jnp.concatenate([proj[:, None]...  19.9 us
    another operation x6, local copies, waits for them, and re-layouts  4.02 us

profile of v1, /device:TPU:1, one launch (start us, length us, event | category | flops | bytes accessed | tf_op | source)
XLA Modules:
  0.0 157.2 jit_solution(17283356431018115579)
XLA Ops:
  0.0 1.4 copy.13.index_ref
  1.4 89.0 %shard_map.64 = f32[2,16,8,256]{3,2,1,0:T(8,128)} custom-call(s32[16,8]{1,0:T(8,128)} %copy.13.index_ref, s32[16]{0:T(128)} %bitcast.58, bf16[2,128,256]{2,1,0:T(8,128)(2,1)} %bitcast.55, bf16[16,8,128,128]{3,2,1,0:T(8,128)(2,1)} %bitcast.49, f32[1,64]{1,0:T(1,128)} %bitcast.59, f32[1,64]{1,0:T(1,128)} %bitcast.60), custom_call_target="tpu_custom_call" | custom-call | tf_op jit(solution)/shard_map/pallas_call | solution.py:331
  90.3 0.8 slice_bitcast_fusion.3
  91.2 0.9 slice_bitcast_fusion
  92.1 0.1 copy.20
  92.2 0.7 slice.100
  92.9 0.1 copy.16
  93.0 0.0 copy-start
  93.0 0.2 maximum_maximum_fusion
  93.2 0.1 copy.15
  93.4 11.7 %cholesky.49 = f32[128,128]{1,0:T(8,128)S(1)} custom-call(f32[128,128]{1,0:T(8,128)S(1)} %cholesky.115), custom_call_target="Cholesky" | custom-call | tf_op jit(solution)/shard_map/jit(cholesky)/cholesky | solution.py:394
  105.2 9.8 %custom-call.18 = f32[1,128,128]{1,2,0:T(8,128)S(1)} custom-call(f32[1,128,128]{2,1,0:T(8,128)S(1)} %get-tuple-element.26), custom_call_target="InvertDiagBlocksLowerTriangular" | custom-call | tf_op jit(solution)/shard_map/jit(cholesky)/cholesky | solution.py:394
  115.0 0.2 constant_dynamic-update-slice_fusion.1
  115.3 0.3 convolution_subtract_fusion.2
  115.5 11.7 %cholesky.103 = f32[128,128]{1,0:T(8,128)S(1)} custom-call(f32[128,128]{1,0:T(8,128)S(1)} %convolution_subtract_fusion.2), custom_call_target="Cholesky" | custom-call | tf_op jit(solution)/shard_map/jit(cholesky)/cholesky | solution.py:394
  127.3 0.7 compare_reduce_fusion
  129.3 0.1 triangular_solve.61
  129.4 4.1 %while.1 = (s32[]{:T(128)}, f32[256,256]{1,0:T(8,128)S(1)}, s32[2,2]{1,0:T(2,128)S(1)}, f32[2,128,128]{2,1,0:T(8,128)S(1)}, s32[]{:T(128)}) while((s32[]{:T(128)}, f32[256,256]{1,0:T(8,128)S(1)}, s32[2,2]{1,0:T(2,128)S(1)}, f32[2,128,128]{2,1,0:T(8,128)S(1)}, s32[]{:T(128)}) %tuple.23), condition=%wide.while_cond, body=%wide.while_body.sunk | while | flops 2 | bytes 131189 | solution.py:395
  129.4 0.7 fusion.33
  130.0 1.3 bitcast_dynamic-update-slice_fusion.2
  131.4 0.7 fusion.33
  132.1 1.3 bitcast_dynamic-update-slice_fusion.2
  133.4 19.9 %custom-call.19 = f32[2,128,128]{1,2,0:T(8,128)S(1)} custom-call(f32[2,128,128]{2,1,0:T(8,128)S(1)} %get-tuple-element.12), custom_call_target="InvertDiagBlocksLowerTriangular" | custom-call | tf_op jit(solution)/shard_map/jit(_cho_solve)/triangular_solve | solution.py:395
  153.3 0.5 fusion.8
  153.8 0.3 convolution_subtract_fusion
  154.1 0.4 fusion.19
  154.5 0.5 fusion.18
  155.0 0.4 convolution_subtract_fusion.1
  155.4 0.3 fusion.17
  155.7 0.1 copy.18
  155.8 0.1 fusion.10
  155.9 0.0 copy-done
  155.9 0.1 convert_reduce_fusion
  156.1 1.2 fusion
  (13 shorter events, 0.2 us)
Async XLA Ops:
  93.0 62.9 %copy-start = (bf16[256,256]{1,0:T(8,128)(2,1)S(1)}, bf16[256,256]{1,0:T(8,128)(2,1)}, u32[]{:S(2)}) copy-start(bf16[256,256]{1,0:T(8,128)(2,1)} %param.6) | copy-start | bytes 393220

commit v2 on v1

--- a/solution.py
+++ b/solution.py
@@ -1,5 +1,3 @@
-import functools
-
 import jax
 import jax.numpy as jnp
 from jax import lax
@@ -11,6 +9,7 @@
 OBS = ("obs_0", "obs_1")
 FLUX = ("flux_0", "flux_1")
 OBS_FLUX = OBS + FLUX
+HIGH = lax.Precision.HIGHEST
 MESH = pl.DeviceIdType.MESH
 F32 = jnp.float32
 BF16 = jnp.bfloat16
@@ -216,7 +215,7 @@
     scaled = (evolved - mean_sim) / sigma
     innovation = (upright(observed_ref[...]) - mean_sim) / sigma
     gram = lax.dot_general(
-        scaled, scaled, (((0,), (0,)), ((), ())), precision=lax.Precision.HIGHEST,
+        scaled, scaled, (((0,), (0,)), ((), ())), precision=HIGH,
         preferred_element_type=F32,
     )
     proj = jnp.sum(innovation * scaled, axis=0, keepdims=True)
@@ -382,25 +381,105 @@
     )
 
 
+def small_inverse(s):
+    n = len(s)
+    if n == 1:
+        return [[1.0 / s[0][0]]]
+    if n == 2:
+        scale = 1.0 / (s[0][0] * s[1][1] - s[0][1] * s[0][1])
+        off = -s[0][1] * scale
+        return [[s[1][1] * scale, off], [off, s[0][0] * scale]]
+    h = n // 2
+    low, high = range(h), range(h, n)
+    e = small_inverse([[s[i][j] for j in low] for i in low])
+    ef = [[sum(e[i][k] * s[k][j] for k in low) for j in high] for i in low]
+    rest = [[s[i][j] - sum(s[k][i] * ef[k][j - h] for k in low) for j in high] for i in high]
+    r = small_inverse(rest)
+    off = [[-sum(ef[i][k] * r[k][j] for k in range(n - h)) for j in range(n - h)] for i in low]
+    top = [[e[i][j] - sum(off[i][k] * ef[j][k] for k in range(n - h)) for j in low] for i in low]
+    out = [[None] * n for _ in range(n)]
+    for i in range(n):
+        for j in range(n):
+            a, b = min(i, j), max(i, j)
+            out[i][j] = top[a][b] if b < h else (off[a][b - h] if a < h else r[a - h][b - h])
+    return out
+
+
+def eliminate(panel, first, m):
+    rows, lanes = panel.shape
+    line = lax.broadcasted_iota(jnp.int32, (rows, 128), 0)
+    column = lax.broadcasted_iota(jnp.int32, (rows, 128), 1)
+    tiles = [panel[:, 128 * t : 128 * t + 128] for t in range(lanes // 128)]
+    home, base = first // 128, first % 128
+    for g in range(0, rows, m):
+        spread = [
+            jnp.broadcast_to(tiles[home][:, base + g + a : base + g + a + 1], (rows, 128)) for a in range(m)
+        ]
+        small = [[spread[b][g + a : g + a + 1] for b in range(m)] for a in range(m)]
+        inverse = small_inverse(small)
+        picked = [[tile[g + a : g + a + 1] for a in range(m)] for tile in tiles]
+        here = column[:1]
+        for a in range(m):
+            at = base + g + a
+            for b in range(m):
+                picked[home][b] = jnp.where(here == at, 1.0 if a == b else 0.0, picked[home][b])
+            tiles[home] = jnp.where(column == at, 0.0, tiles[home])
+        for t in range(len(tiles)):
+            new = [sum(inverse[a][b] * picked[t][b] for b in range(m)) for a in range(m)]
+            value = tiles[t]
+            for a in range(m):
+                value = value - spread[a] * new[a]
+            for a in range(m):
+                value = jnp.where(line == g + a, new[a], value)
+            tiles[t] = value
+    return jnp.concatenate(tiles, axis=1)
+
+
+def posterior_kernel(gram_ref, ensemble_ref, out_ref, full, stack):
+    n, b, m = 256, 64, 4
+    packed_top = gram_ref[0]
+    corner = gram_ref[1]
+    line = lax.broadcasted_iota(jnp.int32, (128, 128), 0)
+    column = lax.broadcasted_iota(jnp.int32, (128, 128), 1)
+    shift = jnp.where(line == column, n - 1.0, 0.0)
+    full[:128, :128] = packed_top[:, :128] + shift
+    full[:128, 128:] = packed_top[:, 128:]
+    full[128:, :128] = packed_top[:, 128:].T
+    full[128:, 128:] = corner[:, :128] + shift
+    proj = jnp.concatenate([corner[:1, 128:], corner[1:2, 128:]], axis=1)
+    lanes = lax.broadcasted_iota(jnp.int32, (n, n), 1)
+    stack[...] = jnp.zeros_like(stack)
+    for k in range(0, n, b):
+        solved = eliminate(full[k : k + b, :], k, m)
+        home, base = k // 128 * 128, k % 128
+        if base == 0:
+            stack[...] = jnp.zeros_like(stack)
+        elif k:
+            stack[base - b : base] = jnp.zeros((b, n), F32)
+        stack[base : base + b] = solved
+        change = jnp.dot(full[:, home : home + 128], stack[...], precision=HIGH, preferred_element_type=F32)
+        full[...] = jnp.where((lanes >= k) & (lanes < k + b), 0.0, full[...]) - change
+        full[k : k + b] = solved
+    inverse = full[...]
+    mean_weights = jnp.sum(inverse * proj, axis=1, keepdims=True)
+    rows = lax.broadcasted_iota(jnp.int32, (n, n), 0)
+    weights = 0.5 * (n - 1.0) * inverse + jnp.where(rows == lanes, 0.5, 0.0) + mean_weights
+    prior = ensemble_ref[...].astype(F32)
+    prior_mean = jnp.mean(prior, axis=1, keepdims=True)
+    moved = jnp.dot(prior - prior_mean, weights, precision=HIGH, preferred_element_type=F32)
+    out_ref[...] = (prior_mean + moved).astype(BF16)
+
+
 def per_device(ensemble, footprint, tile_index, tile_count, observed, obs_sigma):
-    members = ensemble.shape[1]
     packed = summed_gram(ensemble, footprint, tile_index, tile_count, observed, obs_sigma)
-    packed = packed.reshape(2, 128, 256)
-    top, corner = packed[0], packed[1, :, :128]
-    proj = packed[1, :2, 128:].reshape(256)
-    gram = jnp.concatenate([top, jnp.concatenate([top[:, 128:].T, corner], axis=1)], axis=0)
-    eye = jnp.eye(members, dtype=jnp.float32)
-    system = (members - 1.0) * eye + gram
-    factor = jnp.linalg.cholesky(system)
-    solved = jax.scipy.linalg.cho_solve(
-        (factor, True), jnp.concatenate([proj[:, None], gram], axis=1)
-    )
-    weights = eye - 0.5 * solved[:, 1:] + solved[:, 0][:, None]
-    prior = ensemble.astype(jnp.float32)
-    prior_mean = jnp.mean(prior, axis=1)
-    anomaly = prior - prior_mean[:, None]
-    posterior = prior_mean[:, None] + jnp.dot(anomaly, weights, precision=lax.Precision.HIGHEST)
-    return posterior.astype(jnp.bfloat16)
+    vmem = pl.BlockSpec(memory_space=pltpu.VMEM)
+    return pl.pallas_call(
+        posterior_kernel,
+        out_shape=jax.ShapeDtypeStruct((256, 256), BF16),
+        in_specs=[vmem, vmem],
+        out_specs=vmem,
+        scratch_shapes=[pltpu.VMEM((256, 256), F32), pltpu.VMEM((128, 256), F32)],
+    )(packed.reshape(2, 128, 256), ensemble)
 
 
 def solution(mesh):

time: 158 us -> 105 us (0.66)
  other arithmetic: 54.4 us -> 0 us
  Pallas kernels: 89 us -> 104 us
  local copies, waits for them, and re-layouts: 8.41 us -> 1.35 us
  matrix products: 3.99 us -> 0 us
    another operation x9 -> x0, other arithmetic: 53.9 us -> none  [the longest x6 34 us: per_device(): factor = jnp.linalg.cholesky(system)]
    pallas_call x0 -> x1, Pallas kernels: none -> 14.6 us  [per_device(): pl.pallas_call(posterior_kernel, out_shape=jax.ShapeDtypeStruct((256, 256...]
    another operation x11 -> x0, local copies, waits for them, and re-layouts: 4.38 us -> none
    another operation x8 -> x0, matrix products: 2.81 us -> none  [the longest x6 2.34 us: per_device(): jax.scipy.linalg.cho_solve((factor, True), jnp.concatenate([proj[:, None]...]
    squeeze x2 -> x0, local copies, waits for them, and re-layouts: 1.76 us -> none  [per_device(): top, corner = (packed[0], packed[1, :, :128])]
where the time goes in v2:
time: 105 us
  Pallas kernels  104 us (99%)
  local copies, waits for them, and re-layouts  1.35 us (1%)
    pallas_call x1, Pallas kernels, summed_gram(): pl.pallas_call(update_kernel, out_shape=jax.ShapeDtypeStruct((2, Z, 8, 25...  89 us
    pallas_call x1, Pallas kernels, per_device(): pl.pallas_call(posterior_kernel, out_shape=jax.ShapeDtypeStruct((256, 256...  14.6 us

profile of v2, /device:TPU:1, one launch (start us, length us, event | category | flops | bytes accessed | tf_op | source)
XLA Modules:
  0.0 105.0 jit_solution(6449154652701063553)
XLA Ops:
  0.0 1.4 %copy.7.index_ref = s32[16,8]{1,0:T(8,128)} copy(s32[16,8]{0,1:T(8,128)} %bitcast.10) | data formatting | bytes 1024 | tf_op jit(solution)/shard_map/reshape | solution.py:379
  1.4 89.0 %shard_map.64 = f32[2,16,8,256]{3,2,1,0:T(8,128)} custom-call(s32[16,8]{1,0:T(8,128)} %copy.7.index_ref, s32[16]{0:T(128)} %bitcast.11, bf16[2,128,256]{2,1,0:T(8,128)(2,1)} %bitcast.9, bf16[16,8,128,128]{3,2,1,0:T(8,128)(2,1)} %bitcast.7, f32[1,64]{1,0:T(1,128)} %bitcast.12, f32[1,64]{1,0:T(1,128)} %bitcast.13), custom_call_target="tpu_custom_call" | custom-call | tf_op jit(solution)/shard_map/pallas_call | solution.py:330
  90.3 14.6 %shard_map.65 = bf16[256,256]{1,0:T(8,128)(2,1)} custom-call(f32[2,128,256]{2,1,0:T(8,128)} %bitcast.8, bf16[256,256]{1,0:T(8,128)(2,1)} %ensemble_ref.1), custom_call_target="tpu_custom_call" | custom-call | tf_op jit(solution)/shard_map/pallas_call | solution.py:476

commit v3 on v2

--- a/solution.py
+++ b/solution.py
@@ -20,11 +20,11 @@
 def update_kernel(
     index_ref, count_ref, ensemble_ref, footprint_ref, observed_ref, sigma_ref,
     gram_ref,
-    region, prints, part, pair_out, pair_in, right_out, right_in, left_out, left_in,
-    halves, half_in, z_out, z_in, plane_out, plane_in,
-    local_sems, hop_send, hop_recv, pair_send, pair_recv,
-    right_send, right_recv, left_send, left_recv, half_sems,
-    z_send, z_recv, plane_send, plane_recv, share_send, share_recv, give_send, give_recv,
+    region, prints, part, pair_out, pair_in,
+    near_right_out, near_right_in, near_left_out, near_left_in, right_out, right_in, left_out, left_in,
+    halves, half_in, pieces, pieces_in, z_out, z_in,
+    local_sems, hop_send, hop_recv, pair_send, pair_recv, hop_z_send, hop_z_recv, half_sems,
+    scatter_send, scatter_recv, z_send, z_recv, share_send, share_recv, give_send, give_recv,
 ):
     y, x = lax.axis_index("obs_0"), lax.axis_index("obs_1")
     z, c = lax.axis_index("flux_0"), lax.axis_index("flux_1")
@@ -123,25 +123,20 @@
     own.wait()
     load_prints.wait()
 
-    def offset(t):
-        s = t // 2
-        return jnp.where(lax.rem(t, 2) == 0, 8 - s, 9 + s)
-
     def pair_copy(t):
         return pltpu.make_async_remote_copy(
             src_ref=pair_out.at[t], dst_ref=pair_in.at[t], send_sem=pair_send.at[t],
             recv_sem=pair_recv.at[t], device_id=partner, device_id_type=MESH,
         )
 
-    def block(t):
-        b = lax.rem(z + offset(t), Z)
+    def block(t, away):
+        b = lax.rem(z + away + Z, Z)
         count = count_ref[b]
         lhs, rhs = [], []
         for s in range(8):
             values = prints[b, s]
             lhs.append(jnp.where(s < count, values, jnp.zeros_like(values)))
-            at = index_ref[b, s]
-            rhs.append(region[at])
+            rhs.append(region[index_ref[s, b]])
         total = jnp.dot(
             jnp.concatenate(lhs, axis=1), jnp.concatenate(rhs, axis=0), preferred_element_type=F32
         )
@@ -149,60 +144,82 @@
         pair_out[t] = jnp.where(c == 0, total[64:], total[:64]).astype(BF16)
         pair_copy(t).start()
 
-    def right_copy(s):
-        return pltpu.make_async_remote_copy(
-            src_ref=right_out.at[s], dst_ref=right_in.at[s + 1], send_sem=right_send.at[s],
-            recv_sem=right_recv.at[s + 1], device_id=along_z(1), device_id_type=MESH,
-        )
-
-    def left_copy(s):
-        return pltpu.make_async_remote_copy(
-            src_ref=left_out.at[s], dst_ref=left_in.at[s + 1], send_sem=left_send.at[s],
-            recv_sem=left_recv.at[s + 1], device_id=along_z(-1), device_id_type=MESH,
-        )
-
-    right_in[0] = jnp.zeros_like(right_in[0])
-    left_in[0] = jnp.zeros_like(left_in[0])
+    def z_hop(src, dst, k, i, step):
+        return pltpu.make_async_remote_copy(
+            src_ref=src.at[i], dst_ref=dst.at[i], send_sem=hop_z_send.at[k, i],
+            recv_sem=hop_z_recv.at[k, i], device_id=along_z(step), device_id_type=MESH,
+        )
+
+    def near_right(i):
+        return z_hop(near_right_out, near_right_in, 0, i, 1)
+
+    def near_left(i):
+        return z_hop(near_left_out, near_left_in, 1, i, -1)
+
+    def right_copy(i):
+        return z_hop(right_out, right_in, 2, i, 2 - i // 3)
+
+    def left_copy(i):
+        return z_hop(left_out, left_in, 3, i, i // 3 - 2)
 
     def own_sum(t):
         pair_copy(t).wait_recv()
         return part[t] + pair_in[t].astype(F32)
 
-    @pl.loop(0, 9)
-    def _(s):
-        @pl.when(s < 8)
+    @pl.loop(0, 5)
+    def _(i):
+        @pl.when(i < 4)
         def _():
-            block(2 * s)
-            block(2 * s + 1)
-
-        @pl.when(s >= 1)
+            block(4 * i, 8 - 2 * i)
+            block(4 * i + 1, 7 - 2 * i)
+            block(4 * i + 2, 2 * i - 7)
+            block(4 * i + 3, 2 * i - 6)
+            near_right_out[i] = own_sum(4 * i).astype(BF16)
+            near_right(i).start()
+
+        @pl.when(i < 3)
         def _():
-            now = s - 1
-            rightward = own_sum(2 * now)
-
-            @pl.when(now >= 1)
+            near_left_out[i] = own_sum(4 * i + 3).astype(BF16)
+            near_left(i).start()
+
+        @pl.when(i >= 1)
+        def _():
+            n = i - 1
+            left = own_sum(4 * n + 2)
+            right = own_sum(4 * n + 1)
+
+            @pl.when(n == 0)
             def _():
-                right_copy(now - 1).wait_recv()
-
-            right_out[now] = (rightward + right_in[now].astype(F32)).astype(BF16)
-            right_copy(now).start()
-
-            @pl.when(now < 7)
+                left_out[0] = left.astype(BF16)
+
+            @pl.when(n >= 1)
             def _():
-                leftward = own_sum(2 * now + 1)
-
-                @pl.when(now >= 1)
-                def _():
-                    left_copy(now - 1).wait_recv()
-
-                left_out[now] = (leftward + left_in[now].astype(F32)).astype(BF16)
-                left_copy(now).start()
+                near_left(n - 1).wait_recv()
+                left_copy(n - 1).wait_recv()
+                left_out[n] = (
+                    left + near_left_in[n - 1].astype(F32) + left_in[n - 1].astype(F32)
+                ).astype(BF16)
+
+            left_copy(n).start()
+            near_right(n).wait_recv()
+            right = right + near_right_in[n].astype(F32)
+
+            @pl.when(n == 0)
+            def _():
+                right_out[0] = right.astype(BF16)
+
+            @pl.when(n >= 1)
+            def _():
+                right_copy(n - 1).wait_recv()
+                right_out[n] = (right + right_in[n - 1].astype(F32)).astype(BF16)
+
+            right_copy(n).start()
 
     evolved = own_sum(15)
-    left_copy(6).wait_recv()
-    evolved = evolved + left_in[7].astype(F32)
-    right_copy(7).wait_recv()
-    evolved = evolved + right_in[8].astype(F32)
+    left_copy(3).wait_recv()
+    evolved = evolved + left_in[3].astype(F32)
+    right_copy(3).wait_recv()
+    evolved = evolved + right_in[3].astype(F32)
 
     lines = lax.broadcasted_iota(jnp.int32, (64, 64), 0)
     columns = lax.broadcasted_iota(jnp.int32, (64, 64), 1)
@@ -232,12 +249,32 @@
     )
     half_copy.start()
     half_copy.wait_recv()
-    z_out[...] = (halves[c] + half_in[...]).reshape(Z, 8, 256)
+    pieces[...] = (halves[c] + half_in[...]).reshape(16, 8, 256)
+    plane = ((2, 2), (1, 2), (3, 2), (2, 1), (2, 3), (0, 2), (2, 0), (1, 1), (1, 3), (3, 1), (3, 3),
+             (0, 1), (0, 3), (1, 0), (3, 0))
+
+    def spot(dy, dx):
+        at = in_plane(dy, dx)
+        return at[0] * Q + at[1]
+
+    def scatter_copy(t):
+        return pltpu.make_async_remote_copy(
+            src_ref=pieces.at[spot(*plane[t])], dst_ref=pieces_in.at[t], send_sem=scatter_send.at[t],
+            recv_sem=scatter_recv.at[t], device_id=in_plane(*plane[t]), device_id_type=MESH,
+        )
+
+    for t in range(15):
+        scatter_copy(t).start()
+    summed = pieces[mine]
+    for t in reversed(range(15)):
+        scatter_copy(t).wait_recv()
+        summed = summed + pieces_in[t]
+    z_out[...] = summed
 
     def z_copy(t):
-        step = offset(t)
-        return pltpu.make_async_remote_copy(
-            src_ref=z_out.at[lax.rem(z + step, Z)], dst_ref=z_in.at[t], send_sem=z_send.at[t],
+        step = jnp.where(lax.rem(t, 2) == 0, 8 - t // 2, 9 + t // 2)
+        return pltpu.make_async_remote_copy(
+            src_ref=z_out, dst_ref=z_in.at[t], send_sem=z_send.at[t],
             recv_sem=z_recv.at[t], device_id=along_z(step), device_id_type=MESH,
         )
 
@@ -250,29 +287,12 @@
         z_copy(t).wait_recv()
         return total + z_in[t]
 
-    plane_out[...] = lax.fori_loop(0, Z - 1, add_z, z_out[z])
-
-    def plane_copy(t):
-        return pltpu.make_async_remote_copy(
-            src_ref=plane_out, dst_ref=plane_in.at[t], send_sem=plane_send.at[t],
-            recv_sem=plane_recv.at[t], device_id=in_plane(t // Q, lax.rem(t, Q)), device_id_type=MESH,
-        )
-
-    @pl.loop(1, Z)
-    def _(t):
-        plane_copy(t).start()
-
-    def add_plane(t, total):
-        plane_copy(t).wait_recv()
-        return total + plane_in[t]
-
-    whole = lax.fori_loop(1, Z, add_plane, plane_out[...])
-    gram_ref[c, z] = whole
+    gram_ref[c, mine] = lax.fori_loop(0, Z - 1, add_z, summed)
 
     def share_copy(t, at):
         return pltpu.make_async_remote_copy(
             src_ref=gram_ref.at[c, at], dst_ref=gram_ref.at[c, at], send_sem=share_send.at[t],
-            recv_sem=share_recv.at[t], device_id=along_z(offset(t)), device_id_type=MESH,
+            recv_sem=share_recv.at[t], device_id=in_plane(*plane[t]), device_id_type=MESH,
         )
 
     def give_copy(t, half, at):
@@ -281,47 +301,46 @@
             recv_sem=give_recv.at[t], device_id=partner, device_id_type=MESH,
         )
 
-    @pl.loop(0, Z - 1)
-    def _(t):
-        share_copy(t, z).start()
-
-    give_copy(15, c, z).start()
-
-    @pl.loop(0, Z - 1)
-    def _(i):
-        t = Z - 2 - i
-        at = lax.rem(z - offset(t) + Z, Z)
-        share_copy(t, at).wait_recv()
-        give_copy(t, c, at).start()
-
-    @pl.loop(0, Z)
-    def _(i):
-        t = Z - 1 - i
-        at = lax.rem(z - offset(t) + Z, Z)
-        give_copy(t, other, at).wait_recv()
+    def origin(t):
+        dy, dx = plane[t]
+        return spot(-dy, -dx)
+
+    for t in range(15):
+        share_copy(t, mine).start()
+    give_copy(15, c, mine).start()
+    for t in reversed(range(15)):
+        share_copy(t, origin(t)).wait_recv()
+        give_copy(t, c, origin(t)).start()
+    give_copy(15, other, mine).wait_recv()
+    for t in reversed(range(15)):
+        give_copy(t, other, origin(t)).wait_recv()
 
     for copy in sent:
         copy.wait_send()
     half_copy.wait_send()
 
-    @pl.loop(0, Z)
+    @pl.loop(0, 16)
     def _(t):
         pair_copy(t).wait_send()
-        give_copy(t, c, z).wait_send()
-
-    @pl.loop(0, 8)
-    def _(s):
-        right_copy(s).wait_send()
-
-    @pl.loop(0, 7)
-    def _(s):
-        left_copy(s).wait_send()
+        give_copy(t, c, mine).wait_send()
+
+    @pl.loop(0, 4)
+    def _(i):
+        near_right(i).wait_send()
+        right_copy(i).wait_send()
+        left_copy(i).wait_send()
+
+    @pl.loop(0, 3)
+    def _(i):
+        near_left(i).wait_send()
 
     @pl.loop(0, Z - 1)
     def _(t):
         z_copy(t).wait_send()
-        plane_copy(t + 1).wait_send()
-        share_copy(t, z).wait_send()
+
+    for t in range(15):
+        scatter_copy(t).wait_send()
+        share_copy(t, mine).wait_send()
 
 
 def summed_gram(ensemble, footprint, tile_index, tile_count, observed, obs_sigma):
@@ -345,38 +364,28 @@
             vmem((16, 64, 256), F32),
             vmem((16, 64, 256), BF16),
             vmem((16, 64, 256), BF16),
-            vmem((8, 64, 256), BF16),
-            vmem((9, 64, 256), BF16),
-            vmem((7, 64, 256), BF16),
-            vmem((8, 64, 256), BF16),
+            *[vmem((4, 64, 256), BF16)] * 8,
             vmem((2, 128, 256), F32),
             vmem((128, 256), F32),
-            vmem((Z, 8, 256), F32),
-            vmem((Z, 8, 256), F32),
+            vmem((16, 8, 256), F32),
+            vmem((15, 8, 256), F32),
             vmem((8, 256), F32),
-            vmem((Z, 8, 256), F32),
+            vmem((15, 8, 256), F32),
             dma((2,)),
             dma((20,)),
             dma((20,)),
             dma((16,)),
             dma((16,)),
-            dma((8,)),
-            dma((9,)),
-            dma((7,)),
-            dma((8,)),
+            dma((4, 4)),
+            dma((4, 4)),
             dma((2,)),
-            dma((Z,)),
-            dma((Z,)),
-            dma((Z,)),
-            dma((Z,)),
-            dma((Z,)),
-            dma((Z,)),
-            dma((Z,)),
-            dma((Z,)),
+            *[dma((15,))] * 6,
+            dma((16,)),
+            dma((16,)),
         ],
         compiler_params=pltpu.CompilerParams(collective_id=0, has_side_effects=True),
     )(
-        tile_index.reshape(16, 8), tile_count.reshape(16), ensemble.reshape(2, 128, 256),
+        tile_index.reshape(16, 8).T, tile_count.reshape(16), ensemble.reshape(2, 128, 256),
         footprint.reshape(16, 8, 128, 128), observed.reshape(1, 64), obs_sigma.reshape(1, 64),
     )
 

time: 105 us -> 94.5 us (0.900)
  Pallas kernels: 104 us -> 94.3 us
  local copies, waits for them, and re-layouts: 1.35 us -> 0 us
    pallas_call x1, Pallas kernels: 89 us -> 79.7 us  [summed_gram(): pl.pallas_call(update_kernel, out_shape=jax.ShapeDtypeStruct((2, Z, 8, 25...]
    reshape x1 -> x0, local copies, waits for them, and re-layouts: 1.35 us -> none  [summed_gram(): tile_index.reshape(16, 8)]
where the time goes in v3:
time: 94.5 us; the launch traced here: 94.3 us
  Pallas kernels  94.3 us (100%)
    pallas_call x1, Pallas kernels, summed_gram(): pl.pallas_call(update_kernel, out_shape=jax.ShapeDtypeStruct((2, Z, 8, 25...  79.7 us
    pallas_call x1, Pallas kernels, per_device(): pl.pallas_call(posterior_kernel, out_shape=jax.ShapeDtypeStruct((256, 256...  14.6 us

profile of v3, /device:TPU:1, one launch (start us, length us, event | category | flops | bytes accessed | tf_op | source)
XLA Modules:
  0.0 94.3 jit_solution(11622405222396608648)
XLA Ops:
  0.0 79.7 %shard_map.64 = f32[2,16,8,256]{3,2,1,0:T(8,128)} custom-call(s32[8,16]{1,0:T(8,128)} %bitcast.12, s32[16]{0:T(128)} %bitcast.13, bf16[2,128,256]{2,1,0:T(8,128)(2,1)} %bitcast.11, bf16[16,8,128,128]{3,2,1,0:T(8,128)(2,1)} %bitcast.9, f32[1,64]{1,0:T(1,128)} %bitcast.14, f32[1,64]{1,0:T(1,128)} %bitcast.15), custom_call_target="tpu_custom_call" | custom-call | tf_op jit(solution)/shard_map/pallas_call | solution.py:349
  79.7 14.6 %shard_map.65 = bf16[256,256]{1,0:T(8,128)(2,1)} custom-call(f32[2,128,256]{2,1,0:T(8,128)} %bitcast.10, bf16[256,256]{1,0:T(8,128)(2,1)} %ensemble_ref.1), custom_call_target="tpu_custom_call" | custom-call | tf_op jit(solution)/shard_map/pallas_call | solution.py:485

commit v4 on v3

--- a/solution.py
+++ b/solution.py
@@ -24,7 +24,7 @@
     near_right_out, near_right_in, near_left_out, near_left_in, right_out, right_in, left_out, left_in,
     halves, half_in, pieces, pieces_in, z_out, z_in,
     local_sems, hop_send, hop_recv, pair_send, pair_recv, hop_z_send, hop_z_recv, half_sems,
-    scatter_send, scatter_recv, z_send, z_recv, share_send, share_recv, give_send, give_recv,
+    scatter_send, scatter_recv, z_send, z_recv, share_send, share_recv, give_send, give_recv, two_away,
 ):
     y, x = lax.axis_index("obs_0"), lax.axis_index("obs_1")
     z, c = lax.axis_index("flux_0"), lax.axis_index("flux_1")
@@ -51,26 +51,20 @@
     own = pltpu.make_async_copy(ensemble_ref, region.at[pl.ds(2 * mine, 2)], local_sems.at[1])
     own.start()
 
+    ways = (hop(1, 0), hop(-1, 0)), (hop(0, 1), hop(0, -1))
+    near_z = along_z(1), along_z(-1)
     barrier = pltpu.get_barrier_semaphore()
-    pl.semaphore_signal(barrier, inc=1, device_id=partner, device_id_type=MESH)
-
-    @pl.loop(1, Z)
-    def _(step):
-        pl.semaphore_signal(barrier, inc=1, device_id=along_z(step), device_id_type=MESH)
-        pl.semaphore_signal(
-            barrier, inc=1, device_id=in_plane(step // Q, lax.rem(step, Q)), device_id_type=MESH
-        )
-
-    pl.semaphore_wait(barrier, 2 * Z - 1)
+    for to in (partner, *ways[0], *ways[1], *near_z):
+        pl.semaphore_signal(barrier, inc=1, device_id=to, device_id_type=MESH)
+    pl.semaphore_wait(barrier, 7)
+    for k in (0, 1):
+        pl.semaphore_signal(two_away.at[k], inc=1, device_id=near_z[k], device_id_type=MESH)
 
     def piece(src, dst, sem, to):
         return pltpu.make_async_remote_copy(
             src_ref=src, dst_ref=dst, send_sem=hop_send.at[sem], recv_sem=hop_recv.at[sem],
             device_id=to, device_id_type=MESH,
         )
-
-    def arrived(ref, sem):
-        piece(ref, ref, sem, partner).wait_recv()
 
     sent = []
 
@@ -79,47 +73,58 @@
         copy.start()
         sent.append(copy)
 
-    def rows(o):
-        return region.at[pl.ds(2 * o, 2)]
-
-    def tile(o, k):
-        return region.at[2 * o + k]
-
-    forward, back = hop(1, 0), hop(-1, 0)
-    up, down = hop(0, 1), hop(0, -1)
-
-    def rows_at(src, o, k):
-        send(src, rows(o), 4 + 4 * k, up)
-        send(src, rows(o), 5 + 4 * k, down)
-
-    def pass_on(first, k):
-        lower, upper = owner(first, -1), owner(first, 1)
-        arrived(rows(lower), 4 + 4 * k)
-        send(tile(lower, 0), tile(lower, 0), 6 + 4 * k, up)
-        arrived(rows(upper), 5 + 4 * k)
-        send(tile(upper, 1), tile(upper, 1), 7 + 4 * k, down)
-
-    send(ensemble_ref, rows(mine), 0, forward)
-    send(ensemble_ref, rows(mine), 1, back)
-    rows_at(ensemble_ref, mine, 0)
+    def arrived(o, k, sem):
+        piece(region.at[2 * o + k], region.at[2 * o + k], sem, partner).wait_recv()
+
+    firsts = (0, -1, 1, 2)
+
+    def start(src, o, k, axis, way, at):
+        dst = region.at[2 * o + k]
+        send(dst if src is None else src.at[k], dst, 6 * at + 2 * way + k, ways[axis][way])
+
+    def relay(o, axis, way, at):
+        dst = region.at[2 * o + way]
+        send(dst, dst, 6 * at + 4 + way, ways[axis][way])
+
+    def spread(o, k, n):
+        start(None, o, k, 1, 0, 1 + n)
+        start(None, o, k, 1, 1, 1 + n)
+
+    def pass_on(n):
+        for way in (0, 1):
+            o = owner(firsts[n], 2 * way - 1)
+            arrived(o, way, 6 + 6 * n + 3 * way)
+            relay(o, 1, way, 1 + n)
+
+    for turn in (0, 1):
+        for axis in (0, 1):
+            for way in (0, 1):
+                start(ensemble_ref, mine, way if turn == 0 else 1 - way, axis, way, axis)
     behind, ahead, across = owner(-1, 0), owner(1, 0), owner(2, 0)
-    arrived(rows(behind), 0)
-    send(tile(behind, 0), tile(behind, 0), 2, forward)
-    rows_at(rows(behind), behind, 1)
-    arrived(rows(ahead), 1)
-    send(tile(ahead, 1), tile(ahead, 1), 3, back)
-    rows_at(rows(ahead), ahead, 2)
-    pass_on(0, 0)
-    arrived(tile(across, 0), 2)
-    arrived(tile(across, 1), 3)
-    rows_at(rows(across), across, 3)
-    pass_on(-1, 1)
-    pass_on(1, 2)
-    pass_on(2, 3)
-    for k, first in enumerate((0, -1, 1, 2)):
-        far = owner(first, 2)
-        arrived(tile(far, 0), 6 + 4 * k)
-        arrived(tile(far, 1), 7 + 4 * k)
+    arrived(behind, 0, 0)
+    relay(behind, 0, 0, 0)
+    spread(behind, 0, 1)
+    arrived(ahead, 1, 3)
+    relay(ahead, 0, 1, 0)
+    spread(ahead, 1, 2)
+    pass_on(0)
+    arrived(behind, 1, 1)
+    spread(behind, 1, 1)
+    arrived(ahead, 0, 2)
+    spread(ahead, 0, 2)
+    arrived(across, 0, 4)
+    spread(across, 0, 3)
+    arrived(across, 1, 5)
+    spread(across, 1, 3)
+    pass_on(1)
+    pass_on(2)
+    pass_on(3)
+    for n in range(4):
+        lower, upper, far = (owner(firsts[n], k) for k in (-1, 1, 2))
+        arrived(lower, 1, 6 + 6 * n + 1)
+        arrived(upper, 0, 6 + 6 * n + 2)
+        arrived(far, 0, 6 + 6 * n + 4)
+        arrived(far, 1, 6 + 6 * n + 5)
     own.wait()
     load_prints.wait()
 
@@ -129,8 +134,12 @@
             recv_sem=pair_recv.at[t], device_id=partner, device_id_type=MESH,
         )
 
-    def block(t, away):
-        b = lax.rem(z + away + Z, Z)
+    def offset(t):
+        half = t // 2
+        return jnp.where(lax.rem(t, 2) == 0, 8 - half, 9 + half)
+
+    def block(t):
+        b = lax.rem(z + offset(t), Z)
         count = count_ref[b]
         lhs, rhs = [], []
         for s in range(8):
@@ -166,54 +175,55 @@
         pair_copy(t).wait_recv()
         return part[t] + pair_in[t].astype(F32)
 
-    @pl.loop(0, 5)
-    def _(i):
-        @pl.when(i < 4)
-        def _():
-            block(4 * i, 8 - 2 * i)
-            block(4 * i + 1, 7 - 2 * i)
-            block(4 * i + 2, 2 * i - 7)
-            block(4 * i + 3, 2 * i - 6)
-            near_right_out[i] = own_sum(4 * i).astype(BF16)
-            near_right(i).start()
-
-        @pl.when(i < 3)
-        def _():
-            near_left_out[i] = own_sum(4 * i + 3).astype(BF16)
-            near_left(i).start()
-
-        @pl.when(i >= 1)
-        def _():
-            n = i - 1
-            left = own_sum(4 * n + 2)
-            right = own_sum(4 * n + 1)
-
-            @pl.when(n == 0)
-            def _():
-                left_out[0] = left.astype(BF16)
-
-            @pl.when(n >= 1)
-            def _():
-                near_left(n - 1).wait_recv()
-                left_copy(n - 1).wait_recv()
-                left_out[n] = (
-                    left + near_left_in[n - 1].astype(F32) + left_in[n - 1].astype(F32)
-                ).astype(BF16)
-
-            left_copy(n).start()
-            near_right(n).wait_recv()
-            right = right + near_right_in[n].astype(F32)
-
-            @pl.when(n == 0)
-            def _():
-                right_out[0] = right.astype(BF16)
-
-            @pl.when(n >= 1)
-            def _():
-                right_copy(n - 1).wait_recv()
-                right_out[n] = (right + right_in[n - 1].astype(F32)).astype(BF16)
-
-            right_copy(n).start()
+    def blocks(start, stop):
+        @pl.loop(start, stop)
+        def _(t):
+            block(t)
+
+    def near_sends(t):
+        near_left_out[t // 4] = own_sum(t).astype(BF16)
+        near_left(t // 4).start()
+        near_right_out[t // 4 + 1] = own_sum(t + 1).astype(BF16)
+        near_right(t // 4 + 1).start()
+
+    def left_step(i):
+        total = own_sum(4 * i + 1)
+        if i:
+            near_left(i - 1).wait_recv()
+            left_copy(i - 1).wait_recv()
+            total = total + near_left_in[i - 1].astype(F32) + left_in[i - 1].astype(F32)
+        left_out[i] = total.astype(BF16)
+        left_copy(i).start()
+
+    def right_step(i):
+        total = own_sum(4 * i + 2)
+        near_right(i).wait_recv()
+        total = total + near_right_in[i].astype(F32)
+        if i:
+            right_copy(i - 1).wait_recv()
+            total = total + right_in[i - 1].astype(F32)
+        right_out[i] = total.astype(BF16)
+        right_copy(i).start()
+
+    blocks(0, 3)
+    for k in (0, 1):
+        pl.semaphore_wait(two_away.at[k], 1)
+    near_right_out[0] = own_sum(0).astype(BF16)
+    near_right(0).start()
+    left_step(0)
+    blocks(3, 7)
+    near_sends(3)
+    right_step(0)
+    blocks(7, 11)
+    near_sends(7)
+    left_step(1)
+    blocks(11, 16)
+    near_sends(11)
+    right_step(1)
+    left_step(2)
+    right_step(2)
+    left_step(3)
+    right_step(3)
 
     evolved = own_sum(15)
     left_copy(3).wait_recv()
@@ -272,10 +282,9 @@
     z_out[...] = summed
 
     def z_copy(t):
-        step = jnp.where(lax.rem(t, 2) == 0, 8 - t // 2, 9 + t // 2)
         return pltpu.make_async_remote_copy(
             src_ref=z_out, dst_ref=z_in.at[t], send_sem=z_send.at[t],
-            recv_sem=z_recv.at[t], device_id=along_z(step), device_id_type=MESH,
+            recv_sem=z_recv.at[t], device_id=along_z(offset(t)), device_id_type=MESH,
         )
 
     @pl.loop(0, Z - 1)
@@ -372,8 +381,8 @@
             vmem((8, 256), F32),
             vmem((15, 8, 256), F32),
             dma((2,)),
-            dma((20,)),
-            dma((20,)),
+            dma((30,)),
+            dma((30,)),
             dma((16,)),
             dma((16,)),
             dma((4, 4)),
@@ -382,6 +391,7 @@
             *[dma((15,))] * 6,
             dma((16,)),
             dma((16,)),
+            pltpu.SemaphoreType.REGULAR((2,)),
         ],
         compiler_params=pltpu.CompilerParams(collective_id=0, has_side_effects=True),
     )(
@@ -420,31 +430,47 @@
     column = lax.broadcasted_iota(jnp.int32, (rows, 128), 1)
     tiles = [panel[:, 128 * t : 128 * t + 128] for t in range(lanes // 128)]
     home, base = first // 128, first % 128
+    here = column[:1]
+    span = range(m)
+
+    def lifted(top, bottom, lane):
+        return jnp.broadcast_to(tiles[home][top:bottom, lane : lane + 1], (bottom - top, 128))
+
+    small = None
     for g in range(0, rows, m):
-        spread = [
-            jnp.broadcast_to(tiles[home][:, base + g + a : base + g + a + 1], (rows, 128)) for a in range(m)
-        ]
-        small = [[spread[b][g + a : g + a + 1] for b in range(m)] for a in range(m)]
+        at = base + g
+        spread = [lifted(0, rows, at + a) for a in span]
+        if small is None:
+            small = [[spread[b][g + a : g + a + 1] for b in span] for a in span]
         inverse = small_inverse(small)
-        picked = [[tile[g + a : g + a + 1] for a in range(m)] for tile in tiles]
-        here = column[:1]
-        for a in range(m):
-            at = base + g + a
-            for b in range(m):
-                picked[home][b] = jnp.where(here == at, 1.0 if a == b else 0.0, picked[home][b])
-            tiles[home] = jnp.where(column == at, 0.0, tiles[home])
+        if g + m < rows:
+            ahead = [lifted(g, g + 2 * m, at + m + j) for j in span]
+            side = [[ahead[j][b : b + 1] for b in span] for j in span]
+            row = [[sum(inverse[a][b] * side[j][b] for b in span) for j in span] for a in span]
+            small = [[None] * m for _ in span]
+            for i in span:
+                for j in range(i, m):
+                    small[i][j] = ahead[j][m + i : m + i + 1] - sum(side[i][a] * row[a][j] for a in span)
+                    small[j][i] = small[i][j]
+        else:
+            small = None
+        picked = [[tile[g + a : g + a + 1] for a in span] for tile in tiles]
+        for a in span:
+            for b in span:
+                picked[home][b] = jnp.where(here == at + a, 1.0 if a == b else 0.0, picked[home][b])
+        tiles[home] = jnp.where((column >= at) & (column < at + m), 0.0, tiles[home])
         for t in range(len(tiles)):
-            new = [sum(inverse[a][b] * picked[t][b] for b in range(m)) for a in range(m)]
+            new = [sum(inverse[a][b] * picked[t][b] for b in span) for a in span]
             value = tiles[t]
-            for a in range(m):
+            for a in span:
                 value = value - spread[a] * new[a]
-            for a in range(m):
+            for a in span:
                 value = jnp.where(line == g + a, new[a], value)
             tiles[t] = value
     return jnp.concatenate(tiles, axis=1)
 
 
-def posterior_kernel(gram_ref, ensemble_ref, out_ref, full, stack):
+def posterior_kernel(gram_ref, ensemble_ref, out_ref, full):
     n, b, m = 256, 64, 4
     packed_top = gram_ref[0]
     corner = gram_ref[1]
@@ -457,19 +483,21 @@
     full[128:, 128:] = corner[:, :128] + shift
     proj = jnp.concatenate([corner[:1, 128:], corner[1:2, 128:]], axis=1)
     lanes = lax.broadcasted_iota(jnp.int32, (n, n), 1)
-    stack[...] = jnp.zeros_like(stack)
-    for k in range(0, n, b):
-        solved = eliminate(full[k : k + b, :], k, m)
+    panels = [full[k : k + b] for k in range(0, n, b)]
+    lane = lanes[:b]
+    for p in range(n // b):
+        k = p * b
+        solved = eliminate(panels[p], k, m)
         home, base = k // 128 * 128, k % 128
-        if base == 0:
-            stack[...] = jnp.zeros_like(stack)
-        elif k:
-            stack[base - b : base] = jnp.zeros((b, n), F32)
-        stack[base : base + b] = solved
-        change = jnp.dot(full[:, home : home + 128], stack[...], precision=HIGH, preferred_element_type=F32)
-        full[...] = jnp.where((lanes >= k) & (lanes < k + b), 0.0, full[...]) - change
-        full[k : k + b] = solved
-    inverse = full[...]
+        parts = [jnp.zeros((base, n), F32), solved, jnp.zeros((128 - b - base, n), F32)]
+        wide = jnp.concatenate([q for q in parts if q.shape[0]], axis=0)
+        inside = (lane >= k) & (lane < k + b)
+        for step in range(1, n // b):
+            i = (p + step) % (n // b)
+            change = jnp.dot(panels[i][:, home : home + 128], wide, precision=HIGH, preferred_element_type=F32)
+            panels[i] = jnp.where(inside, 0.0, panels[i]) - change
+        panels[p] = solved
+    inverse = jnp.concatenate(panels, axis=0)
     mean_weights = jnp.sum(inverse * proj, axis=1, keepdims=True)
     rows = lax.broadcasted_iota(jnp.int32, (n, n), 0)
     weights = 0.5 * (n - 1.0) * inverse + jnp.where(rows == lanes, 0.5, 0.0) + mean_weights
@@ -487,7 +515,7 @@
         out_shape=jax.ShapeDtypeStruct((256, 256), BF16),
         in_specs=[vmem, vmem],
         out_specs=vmem,
-        scratch_shapes=[pltpu.VMEM((256, 256), F32), pltpu.VMEM((128, 256), F32)],
+        scratch_shapes=[pltpu.VMEM((256, 256), F32)],
     )(packed.reshape(2, 128, 256), ensemble)
 
 

time: 94.5 us -> 84.3 us (0.89)
  Pallas kernels: 94.3 us -> 84.1 us
    pallas_call x1, Pallas kernels: 79.7 us -> 73.8 us  [summed_gram(): pl.pallas_call(update_kernel, out_shape=jax.ShapeDtypeStruct((2, Z, 8, 25...]
    pallas_call x1, Pallas kernels: 14.6 us -> 10.3 us  [per_device(): pl.pallas_call(posterior_kernel, out_shape=jax.ShapeDtypeStruct((256, 256...]
where the time goes in v4:
time: 84.3 us; the launch traced here: 84.1 us
  Pallas kernels  84.1 us (100%)
    pallas_call x1, Pallas kernels, summed_gram(): pl.pallas_call(update_kernel, out_shape=jax.ShapeDtypeStruct((2, Z, 8, 25...  73.8 us
    pallas_call x1, Pallas kernels, per_device(): pl.pallas_call(posterior_kernel, out_shape=jax.ShapeDtypeStruct((256, 256...  10.3 us

profile of v4, /device:TPU:1, one launch (start us, length us, event | category | flops | bytes accessed | tf_op | source)
XLA Modules:
  0.0 84.1 jit_solution(6468764440278981739)
XLA Ops:
  0.0 73.8 %shard_map.64 = f32[2,16,8,256]{3,2,1,0:T(8,128)} custom-call(s32[8,16]{1,0:T(8,128)} %bitcast.12, s32[16]{0:T(128)} %bitcast.13, bf16[2,128,256]{2,1,0:T(8,128)(2,1)} %bitcast.11, bf16[16,8,128,128]{3,2,1,0:T(8,128)(2,1)} %bitcast.9, f32[1,64]{1,0:T(1,128)} %bitcast.14, f32[1,64]{1,0:T(1,128)} %bitcast.15), custom_call_target="tpu_custom_call" | custom-call | tf_op jit(solution)/shard_map/pallas_call | solution.py:358
  73.8 10.3 %shard_map.65 = bf16[256,256]{1,0:T(8,128)(2,1)} custom-call(f32[2,128,256]{2,1,0:T(8,128)} %bitcast.10, bf16[256,256]{1,0:T(8,128)(2,1)} %ensemble_ref.1), custom_call_target="tpu_custom_call" | custom-call | tf_op jit(solution)/shard_map/pallas_call | solution.py:513

commit v5 on v4

--- a/solution.py
+++ b/solution.py
@@ -47,7 +47,6 @@
     mine = y * Q + x
 
     load_prints = pltpu.make_async_copy(footprint_ref, prints, local_sems.at[0])
-    load_prints.start()
     own = pltpu.make_async_copy(ensemble_ref, region.at[pl.ds(2 * mine, 2)], local_sems.at[1])
     own.start()
 
@@ -78,17 +77,17 @@
 
     firsts = (0, -1, 1, 2)
 
-    def start(src, o, k, axis, way, at):
+    def start(o, k, axis, way, at):
         dst = region.at[2 * o + k]
-        send(dst if src is None else src.at[k], dst, 6 * at + 2 * way + k, ways[axis][way])
+        send(dst, dst, 6 * at + 2 * way + k, ways[axis][way])
 
     def relay(o, axis, way, at):
         dst = region.at[2 * o + way]
         send(dst, dst, 6 * at + 4 + way, ways[axis][way])
 
     def spread(o, k, n):
-        start(None, o, k, 1, 0, 1 + n)
-        start(None, o, k, 1, 1, 1 + n)
+        start(o, k, 1, 0, 1 + n)
+        start(o, k, 1, 1, 1 + n)
 
     def pass_on(n):
         for way in (0, 1):
@@ -96,10 +95,12 @@
             arrived(o, way, 6 + 6 * n + 3 * way)
             relay(o, 1, way, 1 + n)
 
+    own.wait()
     for turn in (0, 1):
         for axis in (0, 1):
             for way in (0, 1):
-                start(ensemble_ref, mine, way if turn == 0 else 1 - way, axis, way, axis)
+                start(mine, way if turn == 0 else 1 - way, axis, way, axis)
+    load_prints.start()
     behind, ahead, across = owner(-1, 0), owner(1, 0), owner(2, 0)
     arrived(behind, 0, 0)
     relay(behind, 0, 0, 0)
@@ -125,7 +126,6 @@
         arrived(upper, 0, 6 + 6 * n + 2)
         arrived(far, 0, 6 + 6 * n + 4)
         arrived(far, 1, 6 + 6 * n + 5)
-    own.wait()
     load_prints.wait()
 
     def pair_copy(t):
@@ -219,6 +219,8 @@
     left_step(1)
     blocks(11, 16)
     near_sends(11)
+    for copy in sent:
+        copy.wait_send()
     right_step(1)
     left_step(2)
     right_step(2)
@@ -291,6 +293,25 @@
     def _(t):
         z_copy(t).start()
 
+    half_copy.wait_send()
+
+    @pl.loop(0, 16)
+    def _(t):
+        pair_copy(t).wait_send()
+
+    @pl.loop(0, 4)
+    def _(i):
+        near_right(i).wait_send()
+        right_copy(i).wait_send()
+        left_copy(i).wait_send()
+
+    @pl.loop(0, 3)
+    def _(i):
+        near_left(i).wait_send()
+
+    for t in range(15):
+        scatter_copy(t).wait_send()
+
     def add_z(i, total):
         t = Z - 2 - i
         z_copy(t).wait_recv()
@@ -317,6 +338,11 @@
     for t in range(15):
         share_copy(t, mine).start()
     give_copy(15, c, mine).start()
+
+    @pl.loop(0, Z - 1)
+    def _(t):
+        z_copy(t).wait_send()
+
     for t in reversed(range(15)):
         share_copy(t, origin(t)).wait_recv()
         give_copy(t, c, origin(t)).start()
@@ -324,31 +350,11 @@
     for t in reversed(range(15)):
         give_copy(t, other, origin(t)).wait_recv()
 
-    for copy in sent:
-        copy.wait_send()
-    half_copy.wait_send()
-
     @pl.loop(0, 16)
     def _(t):
-        pair_copy(t).wait_send()
         give_copy(t, c, mine).wait_send()
 
-    @pl.loop(0, 4)
-    def _(i):
-        near_right(i).wait_send()
-        right_copy(i).wait_send()
-        left_copy(i).wait_send()
-
-    @pl.loop(0, 3)
-    def _(i):
-        near_left(i).wait_send()
-
-    @pl.loop(0, Z - 1)
-    def _(t):
-        z_copy(t).wait_send()
-
     for t in range(15):
-        scatter_copy(t).wait_send()
         share_copy(t, mine).wait_send()
 
 

time: 84.3 us -> 83.7 us (level)
  no operation moved by 1% of the time
where the time goes in v5:
time: 83.7 us; the launch traced here: 83.5 us
  Pallas kernels  83.5 us (100%)
    pallas_call x1, Pallas kernels, summed_gram(): pl.pallas_call(update_kernel, out_shape=jax.ShapeDtypeStruct((2, Z, 8, 25...  73.2 us
    pallas_call x1, Pallas kernels, per_device(): pl.pallas_call(posterior_kernel, out_shape=jax.ShapeDtypeStruct((256, 256...  10.3 us

profile of v5, /device:TPU:1, one launch (start us, length us, event | category | flops | bytes accessed | tf_op | source)
XLA Modules:
  0.0 83.5 jit_solution(4306083187774700703)
XLA Ops:
  0.0 73.2 %shard_map.64 = f32[2,16,8,256]{3,2,1,0:T(8,128)} custom-call(s32[8,16]{1,0:T(8,128)} %bitcast.12, s32[16]{0:T(128)} %bitcast.13, bf16[2,128,256]{2,1,0:T(8,128)(2,1)} %bitcast.11, bf16[16,8,128,128]{3,2,1,0:T(8,128)(2,1)} %bitcast.9, f32[1,64]{1,0:T(1,128)} %bitcast.14, f32[1,64]{1,0:T(1,128)} %bitcast.15), custom_call_target="tpu_custom_call" | custom-call | tf_op jit(solution)/shard_map/pallas_call | solution.py:364
  73.2 10.3 %shard_map.65 = bf16[256,256]{1,0:T(8,128)(2,1)} custom-call(f32[2,128,256]{2,1,0:T(8,128)} %bitcast.10, bf16[256,256]{1,0:T(8,128)(2,1)} %ensemble_ref.1), custom_call_target="tpu_custom_call" | custom-call | tf_op jit(solution)/shard_map/pallas_call | solution.py:519
